TPU v7x, 128 devices: a whole 4x4x4 slice. The times are simulated.
128 devices in a mesh: lag: 8 (over y, x_lo), row: 16 (over x_hi, z, core).
Axes of the slice: x: 4 (x_hi: 2, x_lo: 2; x = x_hi * 2 + x_lo), y: 4, z: 4, core: 2. Of those that a mesh axis runs over, the one named last changes fastest.
Arguments:
- lag_weights: float32 [32, 4096, 4096], P('lag', 'row'), may hold values from -0.015625 to 0.015625
- inverse_head: float32 [4096, 4096], P('row'), may hold values from -0.09375 to 0.09375
- excitation: float32 [3, 4096, 128], P(None, 'row'), may hold values from -6 to 6
- history: float32 [32, 4096, 128], P('lag', 'row'), may hold values from -6 to 6
Outputs:
- densities: float32 [3, 4096, 128], P(None, 'row')
All inputs are finite; a program needn't handle non-finite values.
Results may differ from a plain program's by a relative error of at most 0.0001.
Values sent between devices are 32-bit elements; how exact they have to be, the bound alone decides.
A program may use at most 128 MiB of HBM per device.

v0:
```python
import jax
import jax.numpy as jnp
from jax import lax
from jax.sharding import PartitionSpec as P

STEPS = 3


def sent_to_all(shard, axis):
    devices = lax.axis_size(axis)
    return lax.all_to_all(
        jnp.broadcast_to(shard[None], (devices, *shard.shape)), axis, 0, 0, tiled=True
    )


def over_copies(shard, axis):
    return sent_to_all(shard, axis).sum(axis=0)


def in_order(pieces, dim):
    dims = list(pieces.shape[1:])
    dims[dim] *= pieces.shape[0]
    return jnp.moveaxis(pieces, 0, dim).reshape(dims)


def gathered_copies(shard, axis, dim):
    return in_order(sent_to_all(shard, axis), dim)


def from_behind(value, axis, steps):
    count = lax.axis_size(axis)
    leading, last = (max(0, -steps), min(count, count - steps))
    return lax.ppermute(value, axis, [(source, source + steps) for source in range(leading, last)])


def lag_products(weights, piece):
    return jnp.einsum("kmc,kcr->mr", weights, piece, precision=lax.Precision.HIGHEST)


def on_device(lag_weights, inverse_head, excitation, history):
    at_head = lax.axis_index("lag") == 0
    past = lax.all_gather(history, "row", axis=1, tiled=True)
    results = []
    for step in range(STEPS):
        carried = lag_products(lag_weights, past)
        carried = over_copies(carried, "lag")
        right_side = excitation[step] - carried
        density = jnp.dot(
            inverse_head,
            gathered_copies(right_side, "row", 0),
            precision=lax.Precision.HIGHEST,
            preferred_element_type=jnp.float32,
        )
        results.append(density)
        if step + 1 < STEPS:
            whole_density = lax.all_gather(density, "row", axis=0, tiled=True)
            moved = from_behind(past[-1], "lag", 1)
            entering = jnp.where(at_head, whole_density, moved)
            past = jnp.concatenate([entering[None], past[:-1]], axis=0)
    return jnp.stack(results, axis=0)


def solution(mesh):
    placed = (P("lag", "row", None), P("row", None), P(None, "row", None), P("lag", "row", None))
    return jax.shard_map(
        on_device, mesh=mesh, in_specs=placed, out_specs=P(None, "row", None), check_vma=False
    )
```

profile of v0, /device:TPU:1, one launch (start us, length us, event | category | flops | bytes accessed | tf_op | source)
XLA Modules:
  0.0 446.9 jit_solution(8277773772511604061)
XLA Ops:
  6.5 0.0 all-gather.4.cloned.1.call-start
  6.5 0.7 all-gather.4.cloned.1.call-update
  7.3 0.0 all-gather.6.cloned.1.call-start
  7.3 79.4 %all-gather.4.cloned.1.call-done = f32[4,4096,128]{2,1,0:T(8,128)} async-done(((f32[4,256,128]{2,1,0:T(8,128)}), f32[4,4096,128]{2,1,0:T(8,128)}) %all-gather.4.cloned.1.call-update) | async-done | bytes 8388624 | tf_op jit(solution)/shard_map/all_gather | solution.py:42
  86.7 16.8 %convolution_bitcast_fusion.1 = f32[256,128]{1,0:T(8,128)S(1)} fusion(f32[4,256,4096]{2,1,0:T(8,128)} %param.4, f32[4,4096,128]{2,1,0:T(8,128)} %all-gather.4.cloned.1.call-done), kind=kOutput, calls=%fused_computation.16 | convolution fusion | flops 6442450944 | bytes 25296896 | tf_op jit(solution)/shard_map/kmc,kcr->mr/dot_general | solution.py:37
  103.5 0.1 broadcast_in_dim.22
  103.5 18.8 %all_to_all.30 = f32[8,256,128]{2,1,0:T(8,128)S(1)} all-to-all(f32[8,256,128]{2,1,0:T(8,128)S(1)} %broadcast_in_dim.22), channel_id=1, replica_groups=mesh['lag'=8,'row'=16] {'lag'}, dimensions={0} | all-to-all | bytes 2097152 | tf_op jit(solution)/shard_map/all_to_all | solution.py:11
  122.3 0.1 reduce_sum.33
  122.4 0.0 copy-start
  122.4 1.1 fusion.17
  123.5 0.2 broadcast_in_dim.24
  123.7 33.9 %all_to_all.31 = f32[16,256,128]{2,1,0:T(8,128)S(1)} all-to-all(f32[16,256,128]{2,1,0:T(8,128)S(1)} %broadcast_in_dim.24), channel_id=1, replica_groups=mesh['lag'=8,'row'=16] {'row'}, dimensions={0} | all-to-all | bytes 4194304 | tf_op jit(solution)/shard_map/all_to_all | solution.py:11
  157.6 0.0 copy-done
  157.6 4.1 fusion.20
  161.7 0.0 all-gather.6.cloned.1.call-update
  161.7 0.0 all-gather.8.cloned.1.call-start
  161.8 4.5 %slice_bitcast_fusion = (f32[4096,128]{1,0:T(8,128)}, f32[4096,128]{1,0:T(8,128)}) fusion(f32[4,4096,128]{2,1,0:T(8,128)} %all-gather.4.cloned.1.call-done), kind=kLoop, calls=%fused_computation.9 | loop fusion | bytes 8388608 | tf_op jit(solution)/shard_map/squeeze | solution.py:57
  166.3 2.2 collective-permute-start
  168.5 5.9 %slice.30 = f32[3,4096,128]{2,1,0:T(8,128)} slice(f32[4,4096,128]{2,1,0:T(8,128)} %all-gather.4.cloned.1.call-done), slice={[0:3], [0:4096], [0:128]} | slice | bytes 12582912 | tf_op jit(solution)/shard_map/slice | solution.py:59
  174.4 44.9 %collective-permute-done = f32[4096,128]{1,0:T(8,128)S(1)} collective-permute-done((f32[4096,128]{1,0:T(8,128)}, f32[4096,128]{1,0:T(8,128)S(1)}, u32[]{:S(2)}, u32[]{:S(2)}) %collective-permute-start) | collective-permute-done | bytes 2097184 | tf_op jit(solution)/shard_map/ppermute | solution.py:33
  219.3 1.3 copy-done.3
  220.7 1.8 select_bitcast_fusion.1
  222.5 21.1 %fusion.9 = f32[256,128]{0,1:T(8,128)S(1)} fusion(f32[4,256,4096]{2,1,0:T(8,128)} %param.4, f32[3,4096,128]{2,1,0:T(8,128)} %slice.30, f32[1,4096,128]{2,1,0:T(8,128)S(1)} %select_bitcast_fusion.1), kind=kOutput, calls=%fused_computation.13 | convolution fusion | flops 6444548096 | bytes 25296896 | tf_op jit(solution)/shard_map/kmc,kcr->mr/dot_general | solution.py:37
  243.6 0.1 copy.14
  243.7 0.1 broadcast_in_dim.52
  243.7 20.4 %all_to_all.32 = f32[8,256,128]{2,1,0:T(8,128)S(1)} all-to-all(f32[8,256,128]{2,1,0:T(8,128)S(1)} %broadcast_in_dim.52), channel_id=1, replica_groups=mesh['lag'=8,'row'=16] {'lag'}, dimensions={0} | all-to-all | bytes 2097152 | tf_op jit(solution)/shard_map/all_to_all | solution.py:11
  264.1 0.1 reduce_sum.35
  264.2 0.0 copy-start.1
  264.2 1.1 fusion.16
  265.3 0.2 broadcast_in_dim.54
  265.5 33.5 %all_to_all.33 = f32[16,256,128]{2,1,0:T(8,128)S(1)} all-to-all(f32[16,256,128]{2,1,0:T(8,128)S(1)} %broadcast_in_dim.54), channel_id=1, replica_groups=mesh['lag'=8,'row'=16] {'row'}, dimensions={0} | all-to-all | bytes 4194304 | tf_op jit(solution)/shard_map/all_to_all | solution.py:11
  299.0 0.0 copy-done.1
  299.0 4.1 fusion.21
  303.1 0.0 all-gather.8.cloned.1.call-update
  303.1 4.2 collective-permute-start.1
  307.3 49.4 %collective-permute-done.1 = f32[4096,128]{1,0:T(8,128)} collective-permute-done((f32[4096,128]{1,0:T(8,128)}, f32[4096,128]{1,0:T(8,128)}, u32[]{:S(2)}, u32[]{:S(2)}) %collective-permute-start.1) | collective-permute-done | bytes 2097184 | tf_op jit(solution)/shard_map/ppermute | solution.py:33
  356.7 3.1 select_bitcast_fusion
  359.8 21.1 %fusion.12 = f32[256,128]{0,1:T(8,128)S(1)} fusion(f32[4,256,4096]{2,1,0:T(8,128)} %param.4, f32[3,4096,128]{2,1,0:T(8,128)} %slice.30, f32[1,4096,128]{2,1,0:T(8,128)S(1)} %select_bitcast_fusion.1, f32[1,4096,128]{2,1,0:T(8,128)} %select_bitcast_fusion), kind=kOutput, calls=%fused_computation.15 | convolution fusion | flops 6446645248 | bytes 27394048 | tf_op jit(solution)/shard_map/kmc,kcr->mr/dot_general | solution.py:37
  380.9 0.1 copy.17
  381.0 0.1 broadcast_in_dim.56
  381.1 17.9 %all_to_all.34 = f32[8,256,128]{2,1,0:T(8,128)S(1)} all-to-all(f32[8,256,128]{2,1,0:T(8,128)S(1)} %broadcast_in_dim.56), channel_id=1, replica_groups=mesh['lag'=8,'row'=16] {'lag'}, dimensions={0} | all-to-all | bytes 2097152 | tf_op jit(solution)/shard_map/all_to_all | solution.py:11
  399.0 0.1 reduce_sum.37
  399.0 0.0 copy-start.2
  399.0 1.1 fusion.15
  400.1 0.2 broadcast_in_dim.58
  400.3 35.6 %all_to_all.35 = f32[16,256,128]{2,1,0:T(8,128)S(1)} all-to-all(f32[16,256,128]{2,1,0:T(8,128)S(1)} %broadcast_in_dim.58), channel_id=1, replica_groups=mesh['lag'=8,'row'=16] {'row'}, dimensions={0} | all-to-all | bytes 4194304 | tf_op jit(solution)/shard_map/all_to_all | solution.py:11
  435.9 3.4 convolution_bitcast_fusion
  439.4 0.8 pad_maximum_fusion.1
  (8 shorter events, 0.0 us)
Async XLA Ops:
  6.5 80.1 %all-gather.4.cloned.1.call-start = ((), (), s32[]{:S(2)}) async-start(), calls=%async_computation.6 | async-start | bytes 8912896 | tf_op jit(solution)/shard_map/all_gather | solution.py:42
  7.3 213.4 %all-gather.6.cloned.1.call-start = ((), (), s32[]{:S(2)}) async-start(), calls=%async_computation.7 | async-start | bytes 2228224 | tf_op jit(solution)/shard_map/all_gather | solution.py:56
  122.4 35.2 %copy-start = (f32[256,4096]{1,0:T(8,128)S(1)}, f32[256,4096]{1,0:T(8,128)}, u32[]{:S(2)}) copy-start(f32[256,4096]{1,0:T(8,128)} %param.5) | copy-start | bytes 12582916
  161.7 194.9 %all-gather.8.cloned.1.call-start = ((), (), s32[]{:S(2)}) async-start(), calls=%async_computation.8 | async-start | bytes 2228224 | tf_op jit(solution)/shard_map/all_gather | solution.py:56
  166.3 53.0 %collective-permute-start = (f32[4096,128]{1,0:T(8,128)}, f32[4096,128]{1,0:T(8,128)S(1)}, u32[]{:S(2)}, u32[]{:S(2)}) collective-permute-start(f32[4096,128]{1,0:T(8,128)} %get-tuple-element.6), channel_id=1, source_target_pairs={{0,16},{16,32},{32,48},{48,64},{64,80},{80,96},{96,112},{1,17},{17... | collective-permute-start | bytes 6291464 | tf_op jit(solution)/shard_map/ppermute | solution.py:33
  219.3 1.3 copy-start.3
  264.2 34.8 %copy-start.1 = (f32[256,4096]{1,0:T(8,128)S(1)}, f32[256,4096]{1,0:T(8,128)}, u32[]{:S(2)}) copy-start(f32[256,4096]{1,0:T(8,128)} %param.5) | copy-start | bytes 12582916
  303.1 53.5 %collective-permute-start.1 = (f32[4096,128]{1,0:T(8,128)}, f32[4096,128]{1,0:T(8,128)}, u32[]{:S(2)}, u32[]{:S(2)}) collective-permute-start(f32[4096,128]{1,0:T(8,128)} %get-tuple-element.5), channel_id=1, source_target_pairs={{0,16},{16,32},{32,48},{48,64},{64,80},{80,96},{96,112},{1,17},{17... | collective-permute-start | bytes 6291464 | tf_op jit(solution)/shard_map/ppermute | solution.py:33
  399.0 36.9 %copy-start.2 = (f32[256,4096]{1,0:T(8,128)S(1)}, f32[256,4096]{1,0:T(8,128)}, u32[]{:S(2)}) copy-start(f32[256,4096]{1,0:T(8,128)} %param.5) | copy-start | bytes 12582916
  435.9 3.5 copy-start.4
  435.9 3.5 copy-start.5
Sparse Core Ops, SparseCore 0:
  9.9 76.7 all-gather.3
  161.9 49.8 all-gather.5
  303.3 50.0 all-gather.7
where the time goes:
time: 454 us; the launch traced here: 447 us
  waiting for transfers between devices  174 us (38%)
  blocking collectives  160 us (35%)
  matrix products  70.6 us (16%)
  between operations  13.5 us (3%)
  local copies, waits for them, and re-layouts  12.7 us (3%)
  other arithmetic  9.11 us (2%)
  starting transfers between devices  6.42 us (1%)
    all_to_all x6, blocking collectives, sent_to_all(): lax.all_to_all(jnp.broadcast_to(shard[None], (devices, *shard.shape)), ax...  160 us
    ppermute x2, waiting for transfers between devices, from_behind(): lax.ppermute(value, axis, [(source, source + steps) for source in range(l...  94.3 us
    all_gather x1, waiting for transfers between devices, on_device(): past = lax.all_gather(history, 'row', axis=1, tiled=True)  79.4 us
    dot_general x3, matrix products, lag_products(): jnp.einsum('kmc,kcr->mr', weights, piece, precision=lax.Precision.HIGHEST)  58.9 us
    dot_general x3, matrix products, on_device(): jnp.dot(inverse_head, gathered_copies(right_side, 'row', 0), precision=la...  11.7 us
  transfers between devices with their start and end apart: 5, of which 3 were waited for; matrix products, arithmetic and copies ran while one was open for 2% of the time, Pallas kernels for 0%

commit v1 on v0

--- a/solution.py
+++ b/solution.py
@@ -39,7 +39,9 @@
 
 def on_device(lag_weights, inverse_head, excitation, history):
     at_head = lax.axis_index("lag") == 0
-    past = lax.all_gather(history, "row", axis=1, tiled=True)
+    past = jnp.concatenate(
+        lax.all_to_all(jnp.stack([history] * lax.axis_size("row")), "row", 0, 0), axis=1
+    )
     results = []
     for step in range(STEPS):
         carried = lag_products(lag_weights, past)

time: 454 us -> 484 us (1.066); the launches traced: 447 us -> 483 us
  blocking collectives: 160 us -> 266 us
  waiting for transfers between devices: 174 us -> 80.2 us
  local copies, waits for them, and re-layouts: 12.7 us -> 37.2 us
    all_to_all x0 -> x1, blocking collectives: none -> 105 us  [on_device(): lax.all_to_all(jnp.stack([history] * lax.axis_size('row')), 'row', 0, 0)]
    all_gather x1 -> x0, waiting for transfers between devices: 79.4 us -> none  [on_device(): past = lax.all_gather(history, 'row', axis=1, tiled=True)]
    ppermute x2, waiting for transfers between devices: 94.3 us -> 80.2 us  [from_behind(): lax.ppermute(value, axis, [(source, source + steps) for source in range(l...]
    slice x1 -> x3, local copies, waits for them, and re-layouts: 5.89 us -> 20 us  [on_device(): past = jnp.concatenate([entering[None], past[:-1]], axis=0)]
  transfers between devices with their start and end apart: 5 -> 4, of which waited for: 3 -> 2; matrix products, arithmetic and copies ran while one was open for 2% -> 6% of each run, Pallas kernels for 0% -> 0%
where the time goes in v1:
time: 484 us; the launch traced here: 483 us
  blocking collectives  266 us (55%)
  waiting for transfers between devices  80.2 us (17%)
  matrix products  72 us (15%)
  local copies, waits for them, and re-layouts  37.2 us (8%)
  between operations  13.6 us (3%)
  other arithmetic  8.41 us (2%)
  starting transfers between devices  5.76 us (1%)
    all_to_all x6, blocking collectives, sent_to_all(): lax.all_to_all(jnp.broadcast_to(shard[None], (devices, *shard.shape)), ax...  162 us
    all_to_all x1, blocking collectives, on_device(): lax.all_to_all(jnp.stack([history] * lax.axis_size('row')), 'row', 0, 0)  105 us
    ppermute x2, waiting for transfers between devices, from_behind(): lax.ppermute(value, axis, [(source, source + steps) for source in range(l...  80.2 us
    dot_general x3, matrix products, lag_products(): jnp.einsum('kmc,kcr->mr', weights, piece, precision=lax.Precision.HIGHEST)  59.9 us
    slice x3, local copies, waits for them, and re-layouts, on_device(): past = jnp.concatenate([entering[None], past[:-1]], axis=0)  20 us
    dot_general x3, matrix products, on_device(): jnp.dot(inverse_head, gathered_copies(right_side, 'row', 0), precision=la...  12 us
  transfers between devices with their start and end apart: 4, of which 2 were waited for; matrix products, arithmetic and copies ran while one was open for 6% of the time, Pallas kernels for 0%

profile of v1, /device:TPU:1, one launch (start us, length us, event | category | flops | bytes accessed | tf_op | source)
XLA Modules:
  0.0 483.3 jit_solution(8408740098374371930)
XLA Ops:
  6.5 2.1 stack.10
  8.6 104.6 %all_to_all.35 = f32[16,4,256,128]{3,2,1,0:T(8,128)S(1)} all-to-all(f32[16,4,256,128]{3,2,1,0:T(8,128)S(1)} %stack.10), channel_id=1, replica_groups=mesh['lag'=8,'row'=16] {'row'}, dimensions={0} | all-to-all | bytes 16777216 | tf_op jit(solution)/shard_map/all_to_all | solution.py:43
  113.3 1.0 copy.18
  114.2 2.2 copy-done
  116.5 20.0 %convolution_bitcast_fusion.1 = f32[256,128]{1,0:T(8,128)S(1)} fusion(f32[4,256,4096]{2,1,0:T(8,128)} %param.4, f32[4,4096,128]{2,1,0:T(8,128)S(1)} %bitcast.66), kind=kOutput, calls=%fused_computation.14 | convolution fusion | flops 6442450944 | bytes 25296896 | tf_op jit(solution)/shard_map/kmc,kcr->mr/dot_general | solution.py:37
  136.5 0.1 broadcast_in_dim.22
  136.5 18.3 %all_to_all.36 = f32[8,256,128]{2,1,0:T(8,128)S(1)} all-to-all(f32[8,256,128]{2,1,0:T(8,128)S(1)} %broadcast_in_dim.22), channel_id=1, replica_groups=mesh['lag'=8,'row'=16] {'lag'}, dimensions={0} | all-to-all | bytes 2097152 | tf_op jit(solution)/shard_map/all_to_all | solution.py:11
  154.8 0.1 reduce_sum.33
  154.9 1.1 fusion.17
  156.0 0.2 broadcast_in_dim.24
  156.2 34.5 %all_to_all.37 = f32[16,256,128]{2,1,0:T(8,128)S(1)} all-to-all(f32[16,256,128]{2,1,0:T(8,128)S(1)} %broadcast_in_dim.24), channel_id=1, replica_groups=mesh['lag'=8,'row'=16] {'row'}, dimensions={0} | all-to-all | bytes 4194304 | tf_op jit(solution)/shard_map/all_to_all | solution.py:11
  190.7 4.2 fusion.21
  195.0 0.0 all-gather.3.cloned.1.call-update
  195.0 0.0 all-gather.5.cloned.1.call-start
  195.0 4.0 fusion.20
  199.0 1.8 copy.25
  200.8 2.0 collective-permute-start
  202.8 6.2 %slice.36 = f32[3,16,256,128]{3,2,0,1:T(8,128)} slice(f32[4,16,256,128]{3,2,0,1:T(8,128)} %bitcast.65), slice={[0:3], [0:16], [0:256], [0:128]} | slice | bytes 12582912 | tf_op jit(solution)/shard_map/slice | solution.py:61
  209.0 6.7 %copy.20 = f32[3,16,256,128]{2,1,3,0:T(8,128)} copy(f32[3,16,256,128]{3,2,0,1:T(8,128)} %slice.36) | data formatting | bytes 12582912 | tf_op jit(solution)/shard_map/slice | solution.py:61
  215.7 7.2 %slice.31 = f32[3,4096,128]{1,2,0:T(8,128)} reshape(f32[3,16,256,128]{2,1,3,0:T(8,128)} %copy.20) | data formatting | bytes 12582912 | tf_op jit(solution)/shard_map/slice | solution.py:61
  222.9 29.5 %collective-permute-done = f32[4096,128]{0,1:T(8,128)S(1)} collective-permute-done((f32[4096,128]{0,1:T(8,128)}, f32[4096,128]{0,1:T(8,128)S(1)}, u32[]{:S(2)}, u32[]{:S(2)}) %collective-permute-start) | collective-permute-done | bytes 2097184 | tf_op jit(solution)/shard_map/ppermute | solution.py:33
  252.4 1.3 copy-done.4
  253.7 1.8 select_bitcast_fusion.1
  255.5 20.0 %fusion.9 = f32[256,128]{0,1:T(8,128)S(1)} fusion(f32[4,256,4096]{2,1,0:T(8,128)} %param.4, f32[3,4096,128]{1,2,0:T(8,128)} %slice.31, f32[1,4096,128]{1,2,0:T(8,128)S(1)} %select_bitcast_fusion.1), kind=kOutput, calls=%fused_computation.11 | convolution fusion | flops 6444548096 | bytes 25296896 | tf_op jit(solution)/shard_map/kmc,kcr->mr/dot_general | solution.py:37
  275.5 0.1 copy.21
  275.6 0.1 broadcast_in_dim.52
  275.6 20.8 %all_to_all.38 = f32[8,256,128]{2,1,0:T(8,128)S(1)} all-to-all(f32[8,256,128]{2,1,0:T(8,128)S(1)} %broadcast_in_dim.52), channel_id=1, replica_groups=mesh['lag'=8,'row'=16] {'lag'}, dimensions={0} | all-to-all | bytes 2097152 | tf_op jit(solution)/shard_map/all_to_all | solution.py:11
  296.4 0.1 reduce_sum.35
  296.5 0.0 copy-start.2
  296.5 1.1 fusion.16
  297.6 0.2 broadcast_in_dim.54
  297.8 35.3 %all_to_all.39 = f32[16,256,128]{2,1,0:T(8,128)S(1)} all-to-all(f32[16,256,128]{2,1,0:T(8,128)S(1)} %broadcast_in_dim.54), channel_id=1, replica_groups=mesh['lag'=8,'row'=16] {'row'}, dimensions={0} | all-to-all | bytes 4194304 | tf_op jit(solution)/shard_map/all_to_all | solution.py:11
  333.1 4.2 fusion.22
  337.3 0.0 all-gather.5.cloned.1.call-update
  337.3 2.9 copy.26
  340.2 3.7 collective-permute-start.1
  343.9 50.7 %collective-permute-done.1 = f32[4096,128]{0,1:T(8,128)} collective-permute-done((f32[4096,128]{0,1:T(8,128)}, f32[4096,128]{0,1:T(8,128)}, u32[]{:S(2)}, u32[]{:S(2)}) %collective-permute-start.1) | collective-permute-done | bytes 2097184 | tf_op jit(solution)/shard_map/ppermute | solution.py:33
  394.6 3.2 select_bitcast_fusion
  397.8 20.0 %fusion.12 = f32[256,128]{0,1:T(8,128)S(1)} fusion(f32[4,256,4096]{2,1,0:T(8,128)} %param.4, f32[3,4096,128]{1,2,0:T(8,128)} %slice.31, f32[1,4096,128]{1,2,0:T(8,128)S(1)} %select_bitcast_fusion.1, f32[1,4096,128]{1,2,0:T(8,128)} %select_bitcast_fusion), kind=kOutput, calls=%fused_computation.13 | convolution fusion | flops 6446645248 | bytes 27394048 | tf_op jit(solution)/shard_map/kmc,kcr->mr/dot_general | solution.py:37
  417.8 0.1 copy.23
  417.9 0.1 broadcast_in_dim.56
  417.9 17.1 %all_to_all.40 = f32[8,256,128]{2,1,0:T(8,128)S(1)} all-to-all(f32[8,256,128]{2,1,0:T(8,128)S(1)} %broadcast_in_dim.56), channel_id=1, replica_groups=mesh['lag'=8,'row'=16] {'lag'}, dimensions={0} | all-to-all | bytes 2097152 | tf_op jit(solution)/shard_map/all_to_all | solution.py:11
  435.0 0.1 reduce_sum.37
  435.1 1.1 fusion.15
  436.1 0.2 broadcast_in_dim.58
  436.3 35.6 %all_to_all.41 = f32[16,256,128]{2,1,0:T(8,128)S(1)} all-to-all(f32[16,256,128]{2,1,0:T(8,128)S(1)} %broadcast_in_dim.58), channel_id=1, replica_groups=mesh['lag'=8,'row'=16] {'row'}, dimensions={0} | all-to-all | bytes 4194304 | tf_op jit(solution)/shard_map/all_to_all | solution.py:11
  472.0 3.6 convolution_bitcast_fusion
  475.6 0.9 copy.24
  (15 shorter events, 0.1 us)
Async XLA Ops:
  6.5 247.1 %all-gather.3.cloned.1.call-start = ((), (), s32[]{:S(2)}) async-start(), calls=%async_computation.7 | async-start | bytes 2228224 | tf_op jit(solution)/shard_map/all_gather | solution.py:58
  113.3 3.2 copy-start
  154.9 35.8 %copy-start.1 = (f32[256,4096]{1,0:T(8,128)S(1)}, f32[256,4096]{1,0:T(8,128)}, u32[]{:S(2)}) copy-start(f32[256,4096]{1,0:T(8,128)} %param.5) | copy-start | bytes 12582916
  195.0 199.6 %all-gather.5.cloned.1.call-start = ((), (), s32[]{:S(2)}) async-start(), calls=%async_computation.8 | async-start | bytes 2228224 | tf_op jit(solution)/shard_map/all_gather | solution.py:58
  200.8 51.5 %collective-permute-start = (f32[4096,128]{0,1:T(8,128)}, f32[4096,128]{0,1:T(8,128)S(1)}, u32[]{:S(2)}, u32[]{:S(2)}) collective-permute-start(f32[4096,128]{0,1:T(8,128)} %copy.25), channel_id=1, source_target_pairs={{0,16},{16,32},{32,48},{48,64},{64,80},{80,96},{96,112},{1,17},{17... | collective-permute-start | bytes 6291464 | tf_op jit(solution)/shard_map/ppermute | solution.py:33
  252.4 1.3 copy-start.4
  296.5 36.6 %copy-start.2 = (f32[256,4096]{1,0:T(8,128)S(1)}, f32[256,4096]{1,0:T(8,128)}, u32[]{:S(2)}) copy-start(f32[256,4096]{1,0:T(8,128)} %param.5) | copy-start | bytes 12582916
  340.2 54.4 %collective-permute-start.1 = (f32[4096,128]{0,1:T(8,128)}, f32[4096,128]{0,1:T(8,128)}, u32[]{:S(2)}, u32[]{:S(2)}) collective-permute-start(f32[4096,128]{0,1:T(8,128)} %copy.26), channel_id=1, source_target_pairs={{0,16},{16,32},{32,48},{48,64},{64,80},{80,96},{96,112},{1,17},{17... | collective-permute-start | bytes 6291464 | tf_op jit(solution)/shard_map/ppermute | solution.py:33
  435.0 36.9 %copy-start.3 = (f32[256,4096]{1,0:T(8,128)S(1)}, f32[256,4096]{1,0:T(8,128)}, u32[]{:S(2)}) copy-start(f32[256,4096]{1,0:T(8,128)} %param.5) | copy-start | bytes 12582916
  471.9 3.6 copy-start.5
  471.9 3.6 copy-start.6
Sparse Core Ops, SparseCore 0:
  195.1 50.5 all-gather.2
  337.4 50.6 all-gather.4
